TPU v7x, 256 devices: a whole 4x4x8 slice. The times are simulated.
256 devices in a mesh: seq: 8 (over z_lo, x), tensor: 32 (over z_hi, y, core).
Axes of the slice: x: 4, y: 4, z: 8 (z_hi: 4, z_lo: 2; z = z_hi * 2 + z_lo), core: 2. Of those that a mesh axis runs over, the one named last changes fastest.
Arguments:
- tokens: bfloat16 [768, 8192], P('tensor', 'seq'), may hold values from -6 to 6
- w_gate: bfloat16 [8192, 28672], P('seq', 'tensor'), may hold values from -0.109375 to 0.109375
- w_up: bfloat16 [8192, 28672], P('seq', 'tensor'), may hold values from -0.109375 to 0.109375
- w_down: bfloat16 [28672, 8192], P('tensor', 'seq'), may hold values from -0.0546875 to 0.0546875
- mask_gate: int32 [64, 224], P('seq', 'tensor'), may hold values 0 or 1
- mask_up: int32 [64, 224], P('seq', 'tensor'), may hold values 0 or 1
- mask_down: int32 [224, 64], P('tensor', 'seq'), may hold values 0 or 1
- cotangent: bfloat16 [768, 8192], P('tensor', 'seq'), may hold values from -6 to 6
Outputs:
- output: bfloat16 [768, 8192], P('tensor', 'seq')
- grad_tokens: bfloat16 [768, 8192], P('tensor', 'seq')
- grad_gate: bfloat16 [8192, 28672], P('seq', 'tensor')
- grad_up: bfloat16 [8192, 28672], P('seq', 'tensor')
- grad_down: bfloat16 [28672, 8192], P('tensor', 'seq')
All inputs are finite; a program needn't handle non-finite values. No bound on the sum of `mask_gate` or of `mask_up` or of `mask_down` on one device may be relied on, other than what follows from the above.
Results may differ from a plain program's by a relative error of at most 0.0049.
Values may be sent and summed in bfloat16 or wider, within the bound.
A program may use at most 128 MiB of HBM per device.

v0:
```python
import jax
import jax.numpy as jnp
from jax import lax
from jax.sharding import PartitionSpec as P


def widen(mask, rows):
    block = rows // mask.shape[0]
    full = jnp.repeat(jnp.repeat(mask, block, axis=0), block, axis=1)
    return full.astype(jnp.bfloat16)


def gating(summed, width):
    gate = summed[:, :width]
    up = summed[:, width:]
    sig = jax.nn.sigmoid(gate)
    act = gate * sig
    return (gate, up, sig, act)


def gate_up_grads(gate, up, sig, act, grad_hidden):
    dgate = (grad_hidden * up * sig * (1.0 + gate * (1.0 - sig))).astype(jnp.bfloat16)
    dup = (grad_hidden * act).astype(jnp.bfloat16)
    return jnp.concatenate([dgate, dup], axis=1)


def per_device(tokens, w_gate, w_up, w_down, mask_gate, mask_up, mask_down, cotangent):
    width = w_gate.shape[1]
    gate_mask = widen(mask_gate, w_gate.shape[0])
    up_mask = widen(mask_up, w_up.shape[0])
    down_mask = widen(mask_down, w_down.shape[0])
    joined = jnp.concatenate([w_gate * gate_mask, w_up * up_mask], axis=1)
    down_w = w_down * down_mask
    contract_first = (((0,), (0,)), ((), ()))
    contract_last = (((1,), (1,)), ((), ()))
    gathered = lax.all_gather(tokens, "tensor", axis=0, tiled=True)
    partial_value = jnp.dot(gathered, joined, preferred_element_type=jnp.float32)
    summed = lax.psum(partial_value, "seq")
    gate, up, sig, act = gating(summed, width)
    hidden = (act * up).astype(jnp.bfloat16)
    rows_here = hidden
    output = lax.psum_scatter(
        jnp.dot(rows_here, down_w, preferred_element_type=jnp.float32),
        "tensor",
        scatter_dimension=0,
        tiled=True,
    ).astype(jnp.bfloat16)
    cot_rows = lax.all_gather(cotangent, "tensor", axis=0, tiled=True)
    grad_part = lax.dot_general(cot_rows, down_w, contract_last, preferred_element_type=jnp.float32)
    grad_hidden = lax.psum(grad_part, "seq")
    grads = gate_up_grads(gate, up, sig, act, grad_hidden)
    rows_here = grads
    grad_tokens = lax.psum_scatter(
        lax.dot_general(rows_here, joined, contract_last, preferred_element_type=jnp.float32),
        "tensor",
        scatter_dimension=0,
        tiled=True,
    ).astype(jnp.bfloat16)
    weight_grad = lax.dot_general(
        gathered, grads, contract_first, preferred_element_type=jnp.float32
    )
    grad_gate = (weight_grad[:, :width] * gate_mask).astype(jnp.bfloat16)
    grad_up = (weight_grad[:, width:] * up_mask).astype(jnp.bfloat16)
    down_grad = lax.dot_general(
        hidden, cot_rows, contract_first, preferred_element_type=jnp.float32
    )
    grad_down = (down_grad * down_mask).astype(jnp.bfloat16)
    return (output, grad_tokens, grad_gate, grad_up, grad_down)


def solution(mesh):
    return jax.shard_map(
        per_device,
        mesh=mesh,
        in_specs=(
            P("tensor", "seq"),
            P("seq", "tensor"),
            P("seq", "tensor"),
            P("tensor", "seq"),
            P("seq", "tensor"),
            P("seq", "tensor"),
            P("tensor", "seq"),
            P("tensor", "seq"),
        ),
        out_specs=(
            P("tensor", "seq"),
            P("tensor", "seq"),
            P("seq", "tensor"),
            P("seq", "tensor"),
            P("tensor", "seq"),
        ),
        check_vma=False,
    )
```

profile of v0, /device:TPU:4, one launch (start us, length us, event | category | flops | bytes accessed | tf_op | source)
XLA Modules:
  0.0 522.3 jit_solution(15795633586915568263)
XLA Ops:
  7.2 0.0 all-gather.5.cloned.1.call-start
  7.2 0.7 all-gather.5.cloned.1.call-update
  7.9 0.0 all-gather.3.cloned.1.call-start
  7.9 0.7 all-gather.3.cloned.1.call-update
  8.6 0.0 all-reduce.3.cloned.1.call-start
  8.7 0.7 convert_element_type.66
  9.4 0.1 copy.13
  9.5 0.7 convert_element_type.69
  10.2 0.1 copy.15
  10.3 0.7 convert_element_type.73
  11.0 0.1 broadcast_bitcast_fusion
  11.0 0.1 broadcast_bitcast_fusion.1
  11.1 2.9 copy.14
  14.0 3.8 copy.16
  17.8 3.6 bitcast_multiply_fusion
  21.4 45.3 %all-gather.5.cloned.1.call-done = bf16[768,1024]{1,0:T(8,128)(2,1)} async-done(((bf16[24,1024]{1,0:T(8,128)(2,1)}), bf16[768,1024]{1,0:T(8,128)(2,1)}) %all-gather.5.cloned.1.call-update) | async-done | bytes 1572880 | tf_op jit(solution)/shard_map/all_gather | solution.py:48
  66.7 1.1 broadcast_in_dim.23
  67.9 0.0 copy-start.2
  67.9 1.3 copy-done.2
  69.1 0.0 copy-done.7
  69.1 4.7 convolution_bitcast_fusion.2
  73.8 45.8 %all-gather.3.cloned.1.call-done = bf16[768,1024]{1,0:T(8,128)(2,1)} async-done(((bf16[24,1024]{1,0:T(8,128)(2,1)}), bf16[768,1024]{1,0:T(8,128)(2,1)}) %all-gather.3.cloned.1.call-update) | async-done | bytes 1572880 | tf_op jit(solution)/shard_map/all_gather | solution.py:36
  119.6 0.0 copy-done
  119.6 7.5 %convolution_bitcast_fusion.1 = f32[768,1792]{0,1:T(8,128)} fusion(bf16[768,1024]{1,0:T(8,128)(2,1)} %all-gather.3.cloned.1.call-done, bf16[1024,896]{0,1:T(8,128)(2,1)S(1)} %copy-done, bf16[1024,896]{0,1:T(8,128)(2,1)} %get-tuple-element.18), kind=kOutput, calls=%fused_computation.1 | convolution fusion | flops 2825912320 | bytes 10747904 | tf_op jit(solution)/shard_map/dot_general | solution.py:37
  127.1 0.0 all-reduce.3.cloned.1.call-update
  127.1 0.0 reduce-scatter.5.cloned.1.call-start
  127.2 182.2 %all-reduce.3.cloned.1.call-done = (f32[768,1792]{0,1:T(8,128)}, f32[768,896]{0,1:T(8,128)}) async-done(((f32[768,1792]{0,1:T(8,128)}, f32[768,896]{0,1:T(8,128)}), (f32[768,1792]{0,1:T(8,128)}, f32[768,896]{0,1:T(8,128)})) %all-reduce.3.cloned.1.call-update) | async-done | bytes 8257552 | tf_op jit(solution)/shard_map/psum | solution.py:38
  309.4 4.3 multiply_convert_fusion.2
  313.7 0.0 copy-start.4
  313.7 0.0 copy-start.6
  313.7 1.1 copy-done.4
  314.8 0.5 copy-done.6
  315.2 4.8 fusion.3
  320.0 0.0 reduce-scatter.5.cloned.1.call-update
  320.1 0.2 reduce-scatter.3.cloned.1.call-start
  320.3 1.2 copy-done.3
  321.5 5.0 fusion.4
  326.5 0.0 reduce-scatter.3.cloned.1.call-update
  326.5 1.3 copy-done.5
  327.8 4.9 convolution_bitcast_fusion
  332.8 2.4 fusion
  335.2 3.8 copy.18
  339.0 2.4 copy.17
  341.5 4.9 multiply_convert_fusion
  346.3 70.9 %reduce-scatter.5.cloned.1.call-done = f32[24,1024]{1,0:T(8,128)} async-done(((f32[768,1024]{1,0:T(8,128)}), f32[24,1024]{1,0:T(8,128)}) %reduce-scatter.5.cloned.1.call-update) | async-done | bytes 98320 | tf_op jit(solution)/shard_map/reduce_scatter | solution.py:53
  417.3 1.5 convert_element_type.79
  418.8 95.5 %reduce-scatter.3.cloned.1.call-done = f32[24,1024]{1,0:T(8,128)} async-done(((f32[768,1024]{1,0:T(8,128)}), f32[24,1024]{1,0:T(8,128)}) %reduce-scatter.3.cloned.1.call-update) | async-done | bytes 98320 | tf_op jit(solution)/shard_map/reduce_scatter | solution.py:42
  514.2 1.5 convert_element_type.76
  (9 shorter events, 0.1 us)
Async XLA Ops:
  7.2 59.5 %all-gather.5.cloned.1.call-start = ((), (), s32[]{:S(2)}) async-start(), calls=%async_computation.4 | async-start | bytes 1622016 | tf_op jit(solution)/shard_map/all_gather | solution.py:48
  7.9 111.7 %all-gather.3.cloned.1.call-start = ((), (), s32[]{:S(2)}) async-start(), calls=%async_computation.2 | async-start | bytes 1622016 | tf_op jit(solution)/shard_map/all_gather | solution.py:36
  8.6 300.8 %all-reduce.3.cloned.1.call-start = ((), (), s32[]{:S(2)}) async-start(), calls=%async_computation.6 | async-start | bytes 16515072 | tf_op jit(solution)/shard_map/psum | solution.py:38
  66.7 2.4 copy-start.7
  67.9 1.3 copy-start.2
  69.1 50.5 %copy-start = (bf16[1024,896]{0,1:T(8,128)(2,1)S(1)}, bf16[1024,896]{0,1:T(8,128)(2,1)}, u32[]{:S(2)}) copy-start(bf16[1024,896]{0,1:T(8,128)(2,1)} %get-tuple-element.17) | copy-start | bytes 5505028
  127.1 290.2 %reduce-scatter.5.cloned.1.call-start = ((), (), s32[]{:S(2)}) async-start(), calls=%async_computation.5 | async-start | bytes 3244032 | tf_op jit(solution)/shard_map/reduce_scatter | solution.py:53
  309.4 5.8 %copy-start.1 = (bf16[1024,896]{0,1:T(8,128)(2,1)S(1)}, bf16[1024,896]{0,1:T(8,128)(2,1)}, u32[]{:S(2)}) copy-start(bf16[1024,896]{0,1:T(8,128)(2,1)} %get-tuple-element.18) | copy-start | bytes 5505028
  313.7 1.1 copy-start.4
  313.7 1.5 copy-start.6
  320.0 1.5 copy-start.3
  320.1 194.2 %reduce-scatter.3.cloned.1.call-start = ((), (), s32[]{:S(2)}) async-start(), calls=%async_computation.3 | async-start | bytes 3244032 | tf_op jit(solution)/shard_map/reduce_scatter | solution.py:42
  326.5 1.3 copy-start.5
Sparse Core Ops, SparseCore 0:
  10.5 56.1 all-gather.4
  69.2 50.3 all-gather.2
  127.2 182.1 all-reduce.2
  320.2 97.0 reduce-scatter.4
  421.0 93.1 reduce-scatter.2
where the time goes:
time: 523 us; the launch traced here: 522 us
  waiting for transfers between devices  441 us (84%)
  matrix products  31.8 us (6%)
  local copies, waits for them, and re-layouts  19.8 us (4%)
  other arithmetic  15.4 us (3%)
  between operations  13.9 us (3%)
    psum x1, waiting for transfers between devices, per_device(): summed = lax.psum(partial_value, 'seq')  182 us
    reduce_scatter x1, waiting for transfers between devices, per_device(): lax.psum_scatter(jnp.dot(rows_here, down_w, preferred_element_type=jnp.fl...  95.5 us
    reduce_scatter x1, waiting for transfers between devices, per_device(): lax.psum_scatter(lax.dot_general(rows_here, joined, contract_last, prefer...  70.9 us
    all_gather x1, waiting for transfers between devices, per_device(): gathered = lax.all_gather(tokens, 'tensor', axis=0, tiled=True)  45.8 us
    all_gather x1, waiting for transfers between devices, per_device(): cot_rows = lax.all_gather(cotangent, 'tensor', axis=0, tiled=True)  45.3 us
    unnamed x24, local copies, waits for them, and re-layouts  18.5 us
  transfers between devices with their start and end apart: 5, of which 5 were waited for; matrix products, arithmetic and copies ran while one was open for 8% of the time, Pallas kernels for 0%

commit v1 on v0

--- a/solution.py
+++ b/solution.py
@@ -35,7 +35,7 @@
     contract_last = (((1,), (1,)), ((), ()))
     gathered = lax.all_gather(tokens, "tensor", axis=0, tiled=True)
     partial_value = jnp.dot(gathered, joined, preferred_element_type=jnp.float32)
-    summed = lax.psum(partial_value, "seq")
+    summed = jnp.sum(lax.all_gather(partial_value, "seq"), axis=0)
     gate, up, sig, act = gating(summed, width)
     hidden = (act * up).astype(jnp.bfloat16)
     rows_here = hidden

time: 523 us -> 853 us (1.63)
  waiting for transfers between devices: 441 us -> 716 us
  local copies, waits for them, and re-layouts: 19.8 us -> 56.4 us
  other arithmetic: 15.4 us -> 32.7 us
    all_gather x0 -> x1, waiting for transfers between devices: none -> 418 us  [per_device(): summed = jnp.sum(lax.all_gather(partial_value, 'seq'), axis=0)]
    psum x1, waiting for transfers between devices: 182 us -> 40.2 us  [per_device(): grad_hidden = lax.psum(grad_part, 'seq')]
    unnamed x24 -> x27, local copies, waits for them, and re-layouts: 18.5 us -> 55 us
    reduce_sum x0 -> x1, other arithmetic: none -> 18 us  [per_device(): summed = jnp.sum(lax.all_gather(partial_value, 'seq'), axis=0)]
  transfers between devices with their start and end apart: 5 -> 6, of which waited for: 5 -> 6; matrix products, arithmetic and copies ran while one was open for 8% -> 12% of each run, Pallas kernels for 0% -> 0%
where the time goes in v1:
time: 853 us; the launch traced here: 852 us
  waiting for transfers between devices  716 us (84%)
  local copies, waits for them, and re-layouts  56.4 us (7%)
  other arithmetic  32.7 us (4%)
  matrix products  32.1 us (4%)
  between operations  14.2 us (2%)
    all_gather x1, waiting for transfers between devices, per_device(): summed = jnp.sum(lax.all_gather(partial_value, 'seq'), axis=0)  418 us
    reduce_scatter x1, waiting for transfers between devices, per_device(): lax.psum_scatter(jnp.dot(rows_here, down_w, preferred_element_type=jnp.fl...  95.4 us
    reduce_scatter x1, waiting for transfers between devices, per_device(): lax.psum_scatter(lax.dot_general(rows_here, joined, contract_last, prefer...  70.9 us
    unnamed x27, local copies, waits for them, and re-layouts  55 us
    all_gather x1, waiting for transfers between devices, per_device(): gathered = lax.all_gather(tokens, 'tensor', axis=0, tiled=True)  46 us
    all_gather x1, waiting for transfers between devices, per_device(): cot_rows = lax.all_gather(cotangent, 'tensor', axis=0, tiled=True)  44.3 us
    psum x1, waiting for transfers between devices, per_device(): grad_hidden = lax.psum(grad_part, 'seq')  40.2 us
    reduce_sum x1, other arithmetic, per_device(): summed = jnp.sum(lax.all_gather(partial_value, 'seq'), axis=0)  18 us
  transfers between devices with their start and end apart: 6, of which 6 were waited for; matrix products, arithmetic and copies ran while one was open for 12% of the time, Pallas kernels for 0%

profile of v1, /device:TPU:4, one launch (start us, length us, event | category | flops | bytes accessed | tf_op | source)
XLA Modules:
  0.0 852.3 jit_solution(8808661685343007620)
XLA Ops:
  7.2 0.0 all-gather.5.cloned.1.call-start
  7.2 0.7 all-gather.5.cloned.1.call-update
  7.9 0.0 all-gather.7.cloned.1.call-start
  7.9 0.7 all-gather.7.cloned.1.call-update
  8.6 0.0 all-gather.9.cloned.1.call-start
  8.7 0.7 convert_element_type.69
  9.4 0.1 copy.15
  9.5 0.1 broadcast_bitcast_fusion
  9.6 0.7 convert_element_type.66
  10.3 0.1 copy.13
  10.4 0.1 broadcast_bitcast_fusion.1
  10.5 2.9 copy.14
  13.4 3.8 copy.16
  17.1 3.6 bitcast_multiply_fusion
  20.7 46.0 %all-gather.5.cloned.1.call-done = bf16[768,1024]{1,0:T(8,128)(2,1)} async-done(((bf16[24,1024]{1,0:T(8,128)(2,1)}), bf16[768,1024]{1,0:T(8,128)(2,1)}) %all-gather.5.cloned.1.call-update) | async-done | bytes 1572880 | tf_op jit(solution)/shard_map/all_gather | solution.py:36
  66.7 8.0 convolution_bitcast_fusion.1
  74.7 0.0 all-gather.9.cloned.1.call-update
  74.7 0.0 all-reduce.2.cloned.1.call-start
  74.7 0.6 copy-done.7
  75.3 44.3 %all-gather.7.cloned.1.call-done = bf16[768,1024]{1,0:T(8,128)(2,1)} async-done(((bf16[24,1024]{1,0:T(8,128)(2,1)}), bf16[768,1024]{1,0:T(8,128)(2,1)}) %all-gather.7.cloned.1.call-update) | async-done | bytes 1572880 | tf_op jit(solution)/shard_map/all_gather | solution.py:48
  119.6 1.1 broadcast_in_dim.23
  120.8 1.2 copy-done.2
  122.0 4.6 convolution_bitcast_fusion.2
  126.6 0.0 all-reduce.2.cloned.1.call-update
  126.6 0.2 reduce-scatter.5.cloned.1.call-start
  126.9 417.9 %all-gather.9.cloned.1.call-done = f32[6144,1792]{0,1:T(8,128)} async-done(((f32[768,1792]{0,1:T(8,128)}), f32[6144,1792]{0,1:T(8,128)}) %all-gather.9.cloned.1.call-update) | async-done | bytes 44040208 | tf_op jit(solution)/shard_map/all_gather | solution.py:38
  544.8 36.0 %copy.21 = f32[224,8,8,768]{3,2,1,0:T(8,128)} copy(f32[224,8,8,768]{3,1,2,0:T(8,128)} %bitcast.44) | data formatting | bytes 88080384
  580.8 18.0 %bitcast_reduce_fusion = f32[768,1792]{0,1:T(8,128)} fusion(f32[224,8,8,768]{3,2,1,0:T(8,128)} %copy.21), kind=kLoop, calls=%fused_computation | loop fusion | flops 9633792 | bytes 49545216 | tf_op jit(solution)/shard_map/reduce_sum | solution.py:38
  598.9 40.2 %all-reduce.2.cloned.1.call-done = f32[768,896]{0,1:T(8,128)} async-done(((f32[768,896]{0,1:T(8,128)}), f32[768,896]{0,1:T(8,128)}) %all-reduce.2.cloned.1.call-update) | async-done | bytes 2752528 | tf_op jit(solution)/shard_map/psum | solution.py:50
  639.1 4.3 multiply_convert_fusion.2
  643.4 1.1 copy-done.4
  644.5 0.5 copy-done.6
  645.0 4.8 fusion.3
  649.7 0.0 reduce-scatter.5.cloned.1.call-update
  649.8 0.3 reduce-scatter.3.cloned.1.call-start
  650.0 1.2 copy-done.3
  651.2 5.0 fusion.4
  656.2 0.0 reduce-scatter.3.cloned.1.call-update
  656.2 1.3 copy-done.5
  657.6 4.9 convolution_bitcast_fusion
  662.5 2.4 fusion
  664.9 3.8 copy.17
  668.7 2.4 copy.18
  671.2 4.9 multiply_convert_fusion
  676.0 70.9 %reduce-scatter.5.cloned.1.call-done = f32[24,1024]{1,0:T(8,128)} async-done(((f32[768,1024]{1,0:T(8,128)}), f32[24,1024]{1,0:T(8,128)}) %reduce-scatter.5.cloned.1.call-update) | async-done | bytes 98320 | tf_op jit(solution)/shard_map/reduce_scatter | solution.py:53
  746.9 1.5 convert_element_type.79
  748.5 95.4 %reduce-scatter.3.cloned.1.call-done = f32[24,1024]{1,0:T(8,128)} async-done(((f32[768,1024]{1,0:T(8,128)}), f32[24,1024]{1,0:T(8,128)}) %reduce-scatter.3.cloned.1.call-update) | async-done | bytes 98320 | tf_op jit(solution)/shard_map/reduce_scatter | solution.py:42
  843.9 1.5 convert_element_type.76
  (16 shorter events, 0.1 us)
Async XLA Ops:
  7.2 59.5 %all-gather.5.cloned.1.call-start = ((), (), s32[]{:S(2)}) async-start(), calls=%async_computation.2 | async-start | bytes 1622016 | tf_op jit(solution)/shard_map/all_gather | solution.py:36
  7.9 111.7 %all-gather.7.cloned.1.call-start = ((), (), s32[]{:S(2)}) async-start(), calls=%async_computation.4 | async-start | bytes 1622016 | tf_op jit(solution)/shard_map/all_gather | solution.py:48
  8.6 536.2 %all-gather.9.cloned.1.call-start = ((), (), s32[]{:S(2)}) async-start(), calls=%async_computation.7 | async-start | bytes 49545216 | tf_op jit(solution)/shard_map/all_gather | solution.py:38
  74.7 0.7 copy-start.7
  74.7 47.3 %copy-start.8 = (bf16[896,1024]{1,0:T(8,128)(2,1)S(1)}, bf16[896,1024]{1,0:T(8,128)(2,1)}, u32[]{:S(2)}) copy-start(bf16[896,1024]{1,0:T(8,128)(2,1)} %param.11) | copy-start | bytes 5505028
  74.7 564.4 %all-reduce.2.cloned.1.call-start = ((), (), s32[]{:S(2)}) async-start(), calls=%async_computation.5 | async-start | bytes 5505024 | tf_op jit(solution)/shard_map/psum | solution.py:50
  120.8 1.2 copy-start.2
  126.6 620.3 %reduce-scatter.5.cloned.1.call-start = ((), (), s32[]{:S(2)}) async-start(), calls=%async_computation.6 | async-start | bytes 3244032 | tf_op jit(solution)/shard_map/reduce_scatter | solution.py:53
  598.9 46.1 %copy-start = (bf16[1024,896]{0,1:T(8,128)(2,1)S(1)}, bf16[1024,896]{0,1:T(8,128)(2,1)}, u32[]{:S(2)}) copy-start(bf16[1024,896]{0,1:T(8,128)(2,1)} %get-tuple-element.15) | copy-start | bytes 5505028
  639.1 5.8 copy-start.1
  643.4 1.1 copy-start.4
  643.4 1.5 copy-start.6
  649.7 1.5 copy-start.3
  649.8 194.1 %reduce-scatter.3.cloned.1.call-start = ((), (), s32[]{:S(2)}) async-start(), calls=%async_computation.3 | async-start | bytes 3244032 | tf_op jit(solution)/shard_map/reduce_scatter | solution.py:42
  656.2 1.3 copy-start.5
Sparse Core Ops, SparseCore 0:
  10.5 56.1 all-gather.4
  69.2 50.3 all-gather.6
  121.4 423.3 all-gather.8
  547.3 91.7 all-reduce.1
  649.9 97.0 reduce-scatter.4
  750.7 93.1 reduce-scatter.2
